TPU v7x, 256 devices: a whole 4x4x8 slice. The times are simulated.
256 devices in a mesh: ctx: 32 (over y, z), ret: 2 (over core), tp: 4 (over x).
Axes of the slice: x: 4, y: 4, z: 8, core: 2. Of those that a mesh axis runs over, the one named last changes fastest.
Arguments:
- queries: bfloat16 [32768, 2048], P('ctx', 'tp'), may hold values from -256 to 256
- d_attn: bfloat16 [32768, 2048], P('ctx', 'tp'), may hold values from -6 to 6
- pool: bfloat16 [2, 32768, 896], P('ret', 'ctx'), may hold values from -6 to 6
- w_key: bfloat16 [896, 2048], P(None, 'tp'), may hold values from -0.1875 to 0.1875
- w_value: bfloat16 [896, 2048], P(None, 'tp'), may hold values from -0.1875 to 0.1875
- owners: int32 [512, 2], replicated, may hold values from 0 to 31, as said below
- picks: int32 [512, 2], replicated, may hold values from 0 to 1023
- live_counts: int32 [2, 32], replicated, may hold values from 1 to 8
Outputs:
- attn_out: bfloat16 [32768, 2048], P('ctx', 'tp')
- d_queries: bfloat16 [32768, 2048], P('ctx', 'tp')
- d_w_key: bfloat16 [896, 2048], P(None, 'tp')
- d_w_value: bfloat16 [896, 2048], P(None, 'tp')
Inputs may be any that keep to these rules, and one draw needn't show every extreme that they name: `owners`: in each column, at most 1 of the 16 spans of one ctx slab name the same owner, and in every slab some owner is named exactly 1 times.
All inputs are finite; a program needn't handle non-finite values.
Results may differ from a plain program's by a relative error of at most 0.0095.
The roundings to bfloat16 on the way count: a program that leaves them out, or rounds other values in their place, can miss the bound.
Values may be sent and summed in bfloat16 or wider, within the bound.
No kernel may reach another device: no remote copies, remote signals or barrier semaphores. Data moves between devices by JAX's collectives and lax.ppermute only.
A program may use at most 128 MiB of HBM per device.

v0:
```python
import math

import jax
import jax.numpy as jnp
from jax import lax
from jax.sharding import PartitionSpec as P

HEAD_DIM = 128
SPAN = 64
NBR_LEN = 128
CH_DEV = 16


def combined_all(x, axis, combine):
    everything = jax.tree.map(lambda part: lax.all_gather(part, axis), x)
    leading = jax.tree.map(lambda part: part[0], everything)

    def hop(k, so_far):
        return combine(so_far, jax.tree.map(lambda part: part[k], everything))

    return lax.fori_loop(1, lax.axis_size(axis), hop, leading)


def combine_stats(earlier, later):
    first_max, first_total = earlier
    second_max, second_total = later
    joint_max = jnp.maximum(first_max, second_max)
    joint_total = first_total * jnp.exp(first_max - joint_max) + second_total * jnp.exp(
        second_max - joint_max
    )
    return (joint_max, joint_total)


def body(queries, d_attn, pool, w_key, w_value, owners, picks, live_counts):
    ctx_count = lax.axis_size("ctx")
    ctx_place = lax.axis_index("ctx")
    ret_place = lax.axis_index("ret")
    capacity = (CH_DEV + ctx_count - 1) // ctx_count
    head_cols = w_key.shape[1]
    local_heads = head_cols // HEAD_DIM
    blocks = pool.shape[1] // NBR_LEN
    enc_width = pool.shape[2]
    score_scale = 1.0 / math.sqrt(HEAD_DIM)
    owner_col = lax.dynamic_index_in_dim(owners, ret_place, 1, keepdims=False)
    pick_col = lax.dynamic_index_in_dim(picks, ret_place, 1, keepdims=False)
    count_row = lax.dynamic_index_in_dim(live_counts, ret_place, 0, keepdims=False)
    owner_ids = jnp.arange(ctx_count, dtype=jnp.int32)
    counts_of = jnp.sum(
        jnp.where(owner_col[:, None] == owner_ids[None, :], count_row[None, :], 0), axis=1
    )
    slot_col = pick_col % counts_of
    owner_grid = owner_col.reshape(ctx_count, CH_DEV)
    slot_grid = slot_col.reshape(ctx_count, CH_DEV)
    position = jnp.arange(CH_DEV, dtype=jnp.int32)
    earlier = position[None, :] < position[:, None]
    same_owner = owner_grid[:, :, None] == owner_grid[:, None, :]
    request_rank = jnp.sum(jnp.logical_and(same_owner, earlier[None]), axis=2)
    places = jnp.arange(capacity, dtype=jnp.int32)
    wanted = jnp.logical_and(
        (owner_grid == ctx_place)[:, None, :], request_rank[:, None, :] == places[None, :, None]
    )
    send_slot = jnp.sum(jnp.where(wanted, slot_grid[:, None, :], 0), axis=2).reshape(-1)
    send_live = jnp.any(wanted, axis=2).reshape(-1)
    my_owner = lax.dynamic_index_in_dim(owner_grid, ctx_place, 0, keepdims=False)
    my_rank = lax.dynamic_index_in_dim(request_rank, ctx_place, 0, keepdims=False)
    recv_index = my_owner * capacity + my_rank
    pool_blocks = pool[0].reshape(blocks, NBR_LEN, enc_width)
    flat_pool = pool[0]
    own_keys = jnp.dot(flat_pool, w_key, preferred_element_type=jnp.float32).astype(jnp.bfloat16)
    own_values = jnp.dot(flat_pool, w_value, preferred_element_type=jnp.float32).astype(
        jnp.bfloat16
    )
    own_pair = jnp.concatenate([own_keys, own_values], axis=1).reshape(
        blocks, NBR_LEN, 2 * head_cols
    )
    outgoing = jnp.take(own_pair, send_slot, axis=0)
    incoming = lax.all_to_all(outgoing, "ctx", split_axis=0, concat_axis=0, tiled=True)
    chosen = jnp.take(incoming, recv_index, axis=0)
    key_tiles = chosen[:, :, :head_cols]
    value_tiles = chosen[:, :, head_cols:]
    query_tiles = queries.reshape(CH_DEV, SPAN, local_heads, HEAD_DIM)
    grad_out = d_attn.reshape(CH_DEV, SPAN, local_heads, HEAD_DIM)
    key_four = key_tiles.reshape(CH_DEV, NBR_LEN, local_heads, HEAD_DIM)
    value_four = value_tiles.reshape(CH_DEV, NBR_LEN, local_heads, HEAD_DIM)
    scores = (
        jnp.einsum("cmhd,clhd->chml", query_tiles, key_four, preferred_element_type=jnp.float32)
        * score_scale
    )
    local_max = jnp.max(scores, axis=3)
    local_total = jnp.sum(jnp.exp(scores - local_max[..., None]), axis=3)
    row_max, row_total = combined_all((local_max, local_total), "ret", combine_stats)
    attn_prob = jnp.exp(scores - row_max[..., None]) / row_total[..., None]
    prob_bf = attn_prob.astype(jnp.bfloat16)
    partial_value = jnp.einsum(
        "chml,clhd->cmhd", prob_bf, value_four, preferred_element_type=jnp.float32
    )
    attn_full = lax.psum(partial_value.reshape(CH_DEV * SPAN, head_cols), "ret")
    attn_out = attn_full.astype(jnp.bfloat16)
    out_dot = jnp.sum(
        grad_out.astype(jnp.float32)
        * attn_out.reshape(CH_DEV, SPAN, local_heads, HEAD_DIM).astype(jnp.float32),
        axis=3,
    )
    out_dot = jnp.transpose(out_dot, (0, 2, 1))
    grad_prob = jnp.einsum(
        "cmhd,clhd->chml", grad_out, value_four, preferred_element_type=jnp.float32
    )
    dscore = (attn_prob * (grad_prob - out_dot[..., None]) * score_scale).astype(jnp.bfloat16)
    dq_part = jnp.einsum("chml,clhd->cmhd", dscore, key_four, preferred_element_type=jnp.float32)
    d_queries = lax.psum(dq_part.reshape(CH_DEV * SPAN, head_cols), "ret").astype(jnp.bfloat16)
    key_grad = jnp.einsum(
        "chml,cmhd->clhd", dscore, query_tiles, preferred_element_type=jnp.float32
    ).astype(jnp.bfloat16)
    value_grad = jnp.einsum(
        "chml,cmhd->clhd", prob_bf, grad_out, preferred_element_type=jnp.float32
    ).astype(jnp.bfloat16)
    grad_pair = jnp.concatenate(
        [
            key_grad.reshape(CH_DEV, NBR_LEN, head_cols),
            value_grad.reshape(CH_DEV, NBR_LEN, head_cols),
        ],
        axis=2,
    )
    mean_share = 1.0 / (CH_DEV * ctx_count)
    back_hit = recv_index[None, :] == jnp.arange(ctx_count * capacity, dtype=jnp.int32)[:, None]
    back_span = jnp.sum(jnp.where(back_hit, position[None, :], 0), axis=1)
    returning = jnp.take(grad_pair, back_span, axis=0)
    arrived = lax.all_to_all(returning, "ctx", split_axis=0, concat_axis=0, tiled=True)
    arrived = arrived * send_live[:, None, None].astype(jnp.bfloat16)
    source = jnp.take(pool_blocks, send_slot, axis=0).reshape(-1, enc_width)
    weight_part = (
        jnp.einsum(
            "re,rk->ek",
            source,
            arrived.reshape(-1, 2 * head_cols),
            preferred_element_type=jnp.float32,
        )
        * mean_share
    )
    weight_sum = lax.psum(weight_part, ("ctx", "ret"))
    d_w_key = weight_sum[:, :head_cols].astype(jnp.bfloat16)
    d_w_value = weight_sum[:, head_cols:].astype(jnp.bfloat16)
    return (attn_out, d_queries, d_w_key, d_w_value)


def solution(mesh):
    return jax.shard_map(
        body,
        mesh=mesh,
        in_specs=(
            P("ctx", "tp"),
            P("ctx", "tp"),
            P("ret", "ctx", None),
            P(None, "tp"),
            P(None, "tp"),
            P(),
            P(),
            P(),
        ),
        out_specs=(P("ctx", "tp"), P("ctx", "tp"), P(None, "tp"), P(None, "tp")),
        check_vma=False,
    )
```

profile of v0, /device:TPU:2, one launch (start us, length us, event | category | flops | bytes accessed | tf_op | source)
XLA Modules:
  0.0 822.2 jit_solution(8104515446239602236)
XLA Ops:
  10.8 4.0 copy.102
  14.8 6.3 gather_fusion
  21.0 7.5 broadcast_select_fusion.1
  28.5 12.0 %all-to-all-start = ((bf16[32,128,1024]{2,1,0:T(8,128)(2,1)}), bf16[32,128,1024]{2,1,0:T(8,128)(2,1)}, u32[]{:S(2)}, u32[]{:S(2)}) async-start(bf16[32,128,1024]{2,1,0:T(8,128)(2,1)} %broadcast_select_fusion.1), calls=%async_computation | async-start | bytes 16777216 | tf_op jit(solution)/shard_map/all_to_all | solution.py:77
  43.0 185.7 %all-to-all-done = bf16[32,128,1024]{2,1,0:T(8,128)(2,1)} async-done(((bf16[32,128,1024]{2,1,0:T(8,128)(2,1)}), bf16[32,128,1024]{2,1,0:T(8,128)(2,1)}, u32[]{:S(2)}, u32[]{:S(2)}) %all-to-all-start) | async-done | bytes 8388640 | tf_op jit(solution)/shard_map/all_to_all | solution.py:77
  228.7 6.2 gather_fusion.1
  240.1 4.0 copy.82
  244.0 3.9 copy.81
  255.8 3.1 convolution_convert_fusion
  258.8 3.9 copy.95
  268.7 9.9 %all-reduce.3 = bf16[1024,512]{1,0:T(8,128)(2,1)} all-reduce(f32[1024,512]{1,0:T(8,128)} %bitcast.94), channel_id=1, replica_groups=mesh['ctx'=32,'ret'=2,'tp'=4] {'ret'}, use_global_device_ids=true, to_apply=%region_5.6 | all-reduce | flops 524288 | bytes 3145728 | tf_op jit(solution)/shard_map/psum | solution.py:97
  281.3 3.0 multiply_reduce_fusion
  284.6 4.0 fusion.11
  290.7 3.9 copy.94
  294.6 4.8 pad_maximum_fusion
  299.4 7.1 gather_fusion.3
  306.5 7.5 broadcast_select_fusion
  314.0 12.6 %all-to-all-start.1 = ((bf16[32,128,1024]{2,1,0:T(8,128)(2,1)}), bf16[32,128,1024]{2,1,0:T(8,128)(2,1)}, u32[]{:S(2)}, u32[]{:S(2)}) async-start(bf16[32,128,1024]{2,1,0:T(8,128)(2,1)} %broadcast_select_fusion), calls=%async_computation.1 | async-start | bytes 16777216 | tf_op jit(solution)/shard_map/all_to_all | solution.py:128
  326.6 4.4 gather_fusion.2
  330.9 3.1 convolution_bitcast_fusion
  337.0 9.9 %all-reduce.4 = bf16[1024,512]{1,0:T(8,128)(2,1)} all-reduce(f32[1024,512]{1,0:T(8,128)} %bitcast.97), channel_id=1, replica_groups=mesh['ctx'=32,'ret'=2,'tp'=4] {'ret'}, use_global_device_ids=true, to_apply=%region_7.8 | all-reduce | flops 524288 | bytes 3145728 | tf_op jit(solution)/shard_map/psum | solution.py:110
  346.9 169.6 %all-to-all-done.1 = bf16[32,128,1024]{2,1,0:T(8,128)(2,1)} async-done(((bf16[32,128,1024]{2,1,0:T(8,128)(2,1)}), bf16[32,128,1024]{2,1,0:T(8,128)(2,1)}, u32[]{:S(2)}, u32[]{:S(2)}) %all-to-all-start.1) | async-done | bytes 8388640 | tf_op jit(solution)/shard_map/all_to_all | solution.py:128
  516.5 13.8 %bitcast_multiply_fusion = f32[896,1024]{1,0:T(8,128)} fusion(bf16[32,128,1024]{2,1,0:T(8,128)(2,1)} %all-to-all-done.1, bf16[32]{0:T(256)(128)(2,1)S(1)} %convert_element_type.66, bf16[32,128,896]{2,1,0:T(8,128)(2,1)} %gather_fusion.2, pred[32]{0:T(512)(128)(4,1)S(1)} %get-tuple-element.35), kind=kOutput, calls=%fused_computation.13 | convolution fusion | flops 7524974592 | bytes 19398752 | tf_op jit(solution)/shard_map/re,rk->ek/dot_general | solution.py:132
  530.2 289.2 %all-reduce.5 = bf16[896,1024]{1,0:T(8,128)(2,1)} all-reduce(f32[896,1024]{1,0:T(8,128)} %bitcast_multiply_fusion), channel_id=1, replica_groups=mesh['ctx'=32,'ret'=2,'tp'=4] {'ctx','ret'}, use_global_device_ids=true, to_apply=%region_10.11 | all-reduce | flops 917504 | bytes 5505024 | tf_op jit(solution)/shard_map/psum | solution.py:140
  (63 shorter events, 42.2 us)
Async XLA Ops:
  0.6 4.8 copy-start
  5.4 2.6 copy-start.6
  28.5 12.0 %copy-start.5 = (bf16[1024,512]{1,0:T(8,128)(2,1)S(1)}, bf16[1024,512]{1,0:T(8,128)(2,1)}, u32[]{:S(2)}) copy-start(bf16[1024,512]{1,0:T(8,128)(2,1)} %param.9) | copy-start | bytes 3145732
  28.5 200.2 %all-to-all-start = ((bf16[32,128,1024]{2,1,0:T(8,128)(2,1)}), bf16[32,128,1024]{2,1,0:T(8,128)(2,1)}, u32[]{:S(2)}, u32[]{:S(2)}) async-start(bf16[32,128,1024]{2,1,0:T(8,128)(2,1)} %broadcast_select_fusion.1), calls=%async_computation | async-start | bytes 16777216 | tf_op jit(solution)/shard_map/all_to_all | solution.py:77
  250.3 8.5 %copy-start.1 = (f32[16,4,128,64]{2,3,1,0:T(8,128)}, f32[16,4,128,64]{2,3,1,0:T(8,128)S(1)}, u32[]{:S(2)}) copy-start(f32[16,4,128,64]{2,3,1,0:T(8,128)S(1)} %get-tuple-element.33) | copy-start | bytes 6291460
  250.3 5.4 copy-start.2
  288.6 2.1 copy-start.3
  314.0 202.5 %all-to-all-start.1 = ((bf16[32,128,1024]{2,1,0:T(8,128)(2,1)}), bf16[32,128,1024]{2,1,0:T(8,128)(2,1)}, u32[]{:S(2)}, u32[]{:S(2)}) async-start(bf16[32,128,1024]{2,1,0:T(8,128)(2,1)} %broadcast_select_fusion), calls=%async_computation.1 | async-start | bytes 16777216 | tf_op jit(solution)/shard_map/all_to_all | solution.py:128
  326.5 4.4 copy-start.4
where the time goes:
time: 824 us; the launch traced here: 822 us
  waiting for transfers between devices  355 us (43%)
  blocking collectives  313 us (38%)
  local copies, waits for them, and re-layouts  64.2 us (8%)
  matrix products  35.3 us (4%)
  other arithmetic  28.9 us (4%)
  starting transfers between devices  24.6 us (3%)
    psum x1, blocking collectives, body(): weight_sum = lax.psum(weight_part, ('ctx', 'ret'))  289 us
    all_to_all x1, waiting for transfers between devices, body(): lax.all_to_all(outgoing, 'ctx', split_axis=0, concat_axis=0, tiled=True)  186 us
    all_to_all x1, waiting for transfers between devices, body(): lax.all_to_all(returning, 'ctx', split_axis=0, concat_axis=0, tiled=True)  170 us
  transfers between devices with their start and end apart: 2, of which 2 were waited for; matrix products, arithmetic and copies ran while one was open for 2% of the time, Pallas kernels for 0%

commit v1 on v0

v1 whole, which is shorter than its diff:
```python
import math

import jax
import jax.numpy as jnp
from jax import lax
from jax.experimental import pallas as pl
from jax.experimental.pallas import tpu as pltpu
from jax.sharding import Mesh
from jax.sharding import PartitionSpec as P

HEAD_DIM = 128
SPAN = 64
NBR_LEN = 128
CH_DEV = 16
Y_CHIPS = 4

BF16 = jnp.bfloat16
F32 = jnp.float32
ANY = pl.BlockSpec(memory_space=pl.ANY)
SMEM = pl.BlockSpec(memory_space=pltpu.SMEM)


def pack_kernel(slots, place, pool, out, held, in_sem, out_sem):
    part = held.shape[1]
    start = pl.multiple_of(place[0] * part, part)
    load = pltpu.make_async_copy(pool.at[:, pl.ds(start, part), :], held, in_sem)
    load.start()
    load.wait()
    copies = [
        pltpu.make_async_copy(held.at[slots[d]], out.at[d], out_sem.at[d])
        for d in range(out.shape[0])
    ]
    for copy in copies:
        copy.start()
    for copy in copies:
        copy.wait()


def pack(send_slot, tp_place, pool_blocks, part):
    blocks, _, width = pool_blocks.shape
    count = send_slot.shape[0]
    return pl.pallas_call(
        pack_kernel,
        out_shape=jax.ShapeDtypeStruct((count, part, width), BF16),
        in_specs=[SMEM, SMEM, ANY],
        out_specs=ANY,
        scratch_shapes=[
            pltpu.VMEM((blocks, part, width), BF16),
            pltpu.SemaphoreType.DMA,
            pltpu.SemaphoreType.DMA((count,)),
        ],
        name="pack",
    )(send_slot, tp_place, pool_blocks)


def pick_kernel(wanted, incoming, keep, give, held, in_sem, out_sem):
    count = held.shape[0]
    half = count // 2
    loads = [
        pltpu.make_async_copy(incoming.at[wanted[k]], held.at[k], in_sem.at[k])
        for k in range(count)
    ]
    stores = [
        pltpu.make_async_copy(
            held.at[k],
            keep.at[k] if k < half else give.at[k - half],
            out_sem.at[k],
        )
        for k in range(count)
    ]
    for load in loads:
        load.start()
    for k in range(count):
        loads[k].wait()
        stores[k].start()
    for store in stores:
        store.wait()


def pick(wanted, incoming):
    count = wanted.shape[0]
    half = (count // 2,) + incoming.shape[1:]
    return pl.pallas_call(
        pick_kernel,
        out_shape=(jax.ShapeDtypeStruct(half, BF16), jax.ShapeDtypeStruct(half, BF16)),
        in_specs=[SMEM, ANY],
        out_specs=(ANY, ANY),
        scratch_shapes=[
            pltpu.VMEM((count,) + incoming.shape[1:], BF16),
            pltpu.SemaphoreType.DMA((count,)),
            pltpu.SemaphoreType.DMA((count,)),
        ],
        name="pick",
    )(wanted, incoming)


def dot(a, b, dims=((1,), (0,))):
    return lax.dot_general(a, b, (dims, ((), ())), preferred_element_type=F32)


def attend_kernel(
    place,
    gathered,
    queries,
    d_attn,
    w_key,
    w_value,
    attn_out,
    d_queries,
    weight_part,
    rows,
    q_held,
    g_held,
    k_grad,
    v_grad,
    row_sem,
    q_sem,
):
    parts, cols, spans, part, width = gathered.shape
    heads = w_key.shape[1] // HEAD_DIM
    nbr_rows = cols * parts * part
    tokens = spans * SPAN
    scale = 1.0 / math.sqrt(HEAD_DIM)
    me = place[0]
    first = pl.multiple_of(me * tokens, tokens)
    loads = [
        pltpu.make_async_copy(
            gathered.at[p, c],
            rows.at[:, pl.ds((c * parts + p) * part, part), :],
            row_sem.at[c * parts + p],
        )
        for p in range(parts)
        for c in range(cols)
    ] + [
        pltpu.make_async_copy(queries.at[pl.ds(first, tokens), :], q_held, q_sem.at[0]),
        pltpu.make_async_copy(d_attn.at[pl.ds(first, tokens), :], g_held, q_sem.at[1]),
    ]
    for load in loads:
        load.start()
    for load in loads:
        load.wait()

    def span_step(j, carry):
        span_rows = rows[j]
        at = pl.multiple_of(j * SPAN, SPAN)
        to = pl.multiple_of(j * nbr_rows, nbr_rows)
        keys = dot(span_rows, w_key[...]).astype(BF16)
        values = dot(span_rows, w_value[...]).astype(BF16)
        for h in range(heads):
            cut = slice(h * HEAD_DIM, (h + 1) * HEAD_DIM)
            q = q_held[pl.ds(at, SPAN), cut]
            g = g_held[pl.ds(at, SPAN), cut]
            k = keys[:, cut]
            v = values[:, cut]
            scores = dot(q, k, ((1,), (1,))) * scale
            top = jnp.max(scores, axis=1, keepdims=True)
            raised = jnp.exp(scores - top)
            total = jnp.sum(raised, axis=1, keepdims=True)
            prob = raised / total
            prob_b = prob.astype(BF16)
            out = dot(prob_b, v).astype(BF16)
            out_dot = jnp.sum(g.astype(F32) * out.astype(F32), axis=1, keepdims=True)
            grad_prob = dot(g, v, ((1,), (1,)))
            dscore = (prob * (grad_prob - out_dot) * scale).astype(BF16)
            attn_out[pl.ds(at, SPAN), cut] = out
            d_queries[pl.ds(at, SPAN), cut] = dot(dscore, k).astype(BF16)
            k_grad[pl.ds(to, nbr_rows), cut] = dot(dscore, q, ((0,), (0,))).astype(BF16)
            v_grad[pl.ds(to, nbr_rows), cut] = dot(prob_b, g, ((0,), (0,))).astype(BF16)
        return carry

    lax.fori_loop(0, spans, span_step, 0)
    mean_share = 1.0 / (CH_DEV * 32)
    flat = rows[...].reshape(spans * nbr_rows, width)
    for h in range(heads):
        cut = slice(h * HEAD_DIM, (h + 1) * HEAD_DIM)
        weight_part[me, h] = dot(flat, k_grad[:, cut], ((0,), (0,))) * mean_share
        weight_part[1 - me, h] = dot(flat, v_grad[:, cut], ((0,), (0,))) * mean_share


def attend(ret_place, gathered, queries, d_attn, w_key, w_value):
    parts, cols, spans, part, width = gathered.shape
    head_cols = w_key.shape[1]
    tokens = spans * SPAN
    nbr_rows = cols * parts * part
    whole = pl.BlockSpec(memory_space=pltpu.VMEM)
    flops = 2 * spans * nbr_rows * head_cols * (4 * width + 6 * SPAN)
    return pl.pallas_call(
        attend_kernel,
        out_shape=(
            jax.ShapeDtypeStruct((tokens, head_cols), BF16),
            jax.ShapeDtypeStruct((tokens, head_cols), BF16),
            jax.ShapeDtypeStruct((2, head_cols // HEAD_DIM, width, HEAD_DIM), F32),
        ),
        in_specs=[SMEM, ANY, ANY, ANY, whole, whole],
        out_specs=(whole, whole, whole),
        scratch_shapes=[
            pltpu.VMEM((spans, nbr_rows, width), BF16),
            pltpu.VMEM((tokens, head_cols), BF16),
            pltpu.VMEM((tokens, head_cols), BF16),
            pltpu.VMEM((spans * nbr_rows, head_cols), BF16),
            pltpu.VMEM((spans * nbr_rows, head_cols), BF16),
            pltpu.SemaphoreType.DMA((cols * parts,)),
            pltpu.SemaphoreType.DMA((2,)),
        ],
        compiler_params=pltpu.CompilerParams(vmem_limit_bytes=60 * 1024 * 1024),
        cost_estimate=pl.CostEstimate(
            flops=flops, bytes_accessed=12 << 20, transcendentals=spans * SPAN * nbr_rows * 4
        ),
        name="attend",
    )(ret_place, gathered, queries, d_attn, w_key, w_value)


def swap(x):
    return lax.ppermute(x, "ret", [(0, 1), (1, 0)])


def added(x):
    return jnp.sum(x.astype(F32), axis=0).astype(BF16)


def spread(x, axis):
    copies = jnp.broadcast_to(x[None], (lax.axis_size(axis),) + x.shape)
    return lax.all_to_all(copies, axis, split_axis=0, concat_axis=0, tiled=True)


def body(queries, d_attn, pool, w_key, w_value, owners, picks, live_counts):
    y_count = lax.axis_size("y")
    z_count = lax.axis_size("z")
    tp_count = lax.axis_size("tp")
    ctx_count = y_count * z_count
    ctx_place = lax.axis_index("y") * z_count + lax.axis_index("z")
    ret_place = lax.axis_index("ret")
    tp_place = lax.axis_index("tp")
    head_cols = w_key.shape[1]
    heads = head_cols // HEAD_DIM
    width = pool.shape[2]
    part = NBR_LEN // tp_count
    half = CH_DEV // 2
    owner_col = lax.dynamic_index_in_dim(owners, ret_place, 1, keepdims=False)
    pick_col = lax.dynamic_index_in_dim(picks, ret_place, 1, keepdims=False)
    live = live_counts[ret_place, ctx_place]
    owner_grid = owner_col.reshape(ctx_count, CH_DEV)
    pick_grid = pick_col.reshape(ctx_count, CH_DEV)
    asked = jnp.sum(jnp.where(owner_grid == ctx_place, pick_grid, 0), axis=1)
    send_slot = asked % live
    mine = lax.dynamic_slice(owner_col, (ctx_place * CH_DEV + ret_place * half,), (half,))
    others = lax.dynamic_slice(owner_col, (ctx_place * CH_DEV + (1 - ret_place) * half,), (half,))
    wanted = jnp.concatenate([mine, others])

    pool_blocks = pool[0].reshape(-1, NBR_LEN, width)
    outgoing = pack(send_slot, tp_place.reshape(1), pool_blocks, part)
    incoming = lax.all_to_all(outgoing, ("y", "z"), split_axis=0, concat_axis=0, tiled=True)
    keep, give = pick(wanted, incoming)
    got = swap(give)
    gathered = lax.all_gather(jnp.stack([keep, got]), "tp")
    attn_half, dq_half, weight_part = attend(
        ret_place.reshape(1), gathered, queries, d_attn, w_key, w_value
    )
    pair = (weight_part[0] + swap(weight_part[1])).astype(BF16)
    by_y = added(lax.all_to_all(pair, "y", split_axis=0, concat_axis=0, tiled=False))
    by_y = by_y.reshape(z_count, width // z_count, HEAD_DIM)
    by_z = added(lax.all_to_all(by_y, "z", split_axis=0, concat_axis=0, tiled=False))
    z_full = spread(by_z, "z").reshape(width, HEAD_DIM)
    mine_full = spread(z_full, "y").reshape(heads, width, HEAD_DIM)
    other_full = swap(mine_full)
    low = ret_place == 0
    d_w_key = jnp.where(low, mine_full, other_full)
    d_w_value = jnp.where(low, other_full, mine_full)
    d_w_key = jnp.transpose(d_w_key, (1, 0, 2)).reshape(width, head_cols)
    d_w_value = jnp.transpose(d_w_value, (1, 0, 2)).reshape(width, head_cols)

    def joined(x):
        y = swap(x)
        return jnp.concatenate([jnp.where(low, x, y), jnp.where(low, y, x)], axis=0)

    return (joined(attn_half), joined(dq_half), d_w_key, d_w_value)


def solution(mesh):
    shape = (Y_CHIPS, mesh.shape["ctx"] // Y_CHIPS, mesh.shape["ret"], mesh.shape["tp"])
    fine = Mesh(mesh.devices.reshape(shape), ("y", "z", "ret", "tp"))
    ctx = ("y", "z")
    return jax.shard_map(
        body,
        mesh=fine,
        in_specs=(
            P(ctx, "tp"),
            P(ctx, "tp"),
            P("ret", ctx, None),
            P(None, "tp"),
            P(None, "tp"),
            P(),
            P(),
            P(),
        ),
        out_specs=(P(ctx, "tp"), P(ctx, "tp"), P(None, "tp"), P(None, "tp")),
        check_vma=False,
    )
```

time: 824 us -> 248 us (0.30)
  blocking collectives: 313 us -> 47.7 us
  waiting for transfers between devices: 355 us -> 102 us
  local copies, waits for them, and re-layouts: 64.2 us -> 9.47 us
  Pallas kernels: 0 us -> 44.9 us
  matrix products: 35.3 us -> 0 us
  other arithmetic: 28.9 us -> 9.17 us
  between operations: 0.92 us -> 15.5 us
  starting transfers between devices: 24.6 us -> 15.9 us
    psum x3 -> x0, blocking collectives: 309 us -> none  [the longest x1 289 us: body(): weight_sum = lax.psum(weight_part, ('ctx', 'ret'))]
    all_to_all x2, waiting for transfers between devices: 355 us -> 52.9 us  [the longest x1 43.2 us: body(): lax.all_to_all(outgoing, ('y', 'z'), split_axis=0, concat_axis=0, tiled=T...]
    all_to_all x0 -> x3, blocking collectives: none -> 47.7 us  [the longest x1 18.1 us: body(): lax.all_to_all(pair, 'y', split_axis=0, concat_axis=0, tiled=False)]
    pallas_call x0 -> x3, Pallas kernels: none -> 44.9 us  [the longest x1 38.9 us: attend(): pl.pallas_call(attend_kernel, out_shape=(jax.ShapeDtypeStruct((tokens, he...]
    all_gather x0 -> x1, waiting for transfers between devices: none -> 43.2 us  [body(): gathered = lax.all_gather(jnp.stack([keep, got]), 'tp')]
    dot_general x9 -> x0, matrix products: 35.3 us -> none  [the longest x1 13.8 us: body(): jnp.einsum('re,rk->ek', source, arrived.reshape(-1, 2 * head_cols), prefe...]
    gather x4 -> x0, local copies, waits for them, and re-layouts: 23.9 us -> none  [the longest x1 7.1 us: body(): returning = jnp.take(grad_pair, back_span, axis=0)]
    reshape x7 -> x0, local copies, waits for them, and re-layouts: 14.4 us -> none  [the longest x1 3.95 us: body(): jnp.concatenate([own_keys, own_values], axis=1)]
  transfers between devices with their start and end apart: 2 -> 8, of which waited for: 2 -> 5; matrix products, arithmetic and copies ran while one was open for 2% -> 2% of each run, Pallas kernels for 0% -> 0%
where the time goes in v1:
time: 248 us; the launch traced here: 245 us
  waiting for transfers between devices  102 us (41%)
  blocking collectives  47.7 us (19%)
  Pallas kernels  44.9 us (18%)
  starting transfers between devices  15.9 us (6%)
  between operations  15.5 us (6%)
  local copies, waits for them, and re-layouts  9.47 us (4%)
  other arithmetic  9.17 us (4%)
    all_to_all x1, waiting for transfers between devices, body(): lax.all_to_all(outgoing, ('y', 'z'), split_axis=0, concat_axis=0, tiled=T...  43.2 us
    all_gather x1, waiting for transfers between devices, body(): gathered = lax.all_gather(jnp.stack([keep, got]), 'tp')  43.2 us
    pallas_call x1, Pallas kernels, attend(): pl.pallas_call(attend_kernel, out_shape=(jax.ShapeDtypeStruct((tokens, he...  38.9 us
    all_to_all x1, blocking collectives, body(): lax.all_to_all(pair, 'y', split_axis=0, concat_axis=0, tiled=False)  18.1 us
    all_to_all x1, blocking collectives, body(): lax.all_to_all(by_y, 'z', split_axis=0, concat_axis=0, tiled=False)  17.1 us
    all_to_all x1, blocking collectives, spread(): return lax.all_to_all(copies, axis, split_axis=0, concat_axis=0, tiled=True)  12.5 us
    all_to_all x1, starting transfers between devices, body(): lax.all_to_all(outgoing, ('y', 'z'), split_axis=0, concat_axis=0, tiled=T...  11.5 us
    all_to_all x1, waiting for transfers between devices, spread(): return lax.all_to_all(copies, axis, split_axis=0, concat_axis=0, tiled=True)  9.74 us
  transfers between devices with their start and end apart: 8, of which 5 were waited for; matrix products, arithmetic and copies ran while one was open for 2% of the time, Pallas kernels for 0%

profile of v1, /device:TPU:2, one launch (start us, length us, event | category | flops | bytes accessed | tf_op | source)
XLA Modules:
  0.0 244.6 jit_solution(3547099955593770210)
XLA Ops:
  7.2 1.3 dynamic_slice.26
  11.3 3.2 %pack.1 = bf16[32,32,896]{2,1,0:T(8,128)(2,1)} custom-call(s32[32]{0:T(128)} %and_select_fusion.slots, s32[1]{0:T(128)} %bitcast.4.place, bf16[8,128,896]{2,1,0:T(8,128)(2,1)} %bitcast.27), custom_call_target="tpu_custom_call" | custom-call | tf_op jit(solution)/shard_map/pack/pallas_call | solution.py:42
  14.6 11.5 %all-to-all-start = ((bf16[32,32,896]{2,1,0:T(8,128)(2,1)}), bf16[32,32,896]{2,1,0:T(8,128)(2,1)S(1)}, u32[]{:S(2)}, u32[]{:S(2)}) async-start(bf16[32,32,896]{2,1,0:T(8,128)(2,1)} %pack.1), calls=%async_computation | async-start | bytes 3670016 | tf_op jit(solution)/shard_map/all_to_all | solution.py:252
  27.6 43.2 %all-to-all-done.incoming = bf16[32,32,896]{2,1,0:T(8,128)(2,1)S(1)} async-done(((bf16[32,32,896]{2,1,0:T(8,128)(2,1)}), bf16[32,32,896]{2,1,0:T(8,128)(2,1)S(1)}, u32[]{:S(2)}, u32[]{:S(2)}) %all-to-all-start) | async-done | bytes 1835040 | tf_op jit(solution)/shard_map/all_to_all | solution.py:252
  70.8 1.3 copy-done
  72.0 2.8 %pick.1 = (bf16[8,32,896]{2,1,0:T(8,128)(2,1)}, bf16[8,32,896]{2,1,0:T(8,128)(2,1)}) custom-call(s32[16]{0:T(128)} %pad_add_fusion.wanted, bf16[32,32,896]{2,1,0:T(8,128)(2,1)} %copy-done), custom_call_target="tpu_custom_call" | custom-call | tf_op jit(solution)/shard_map/pick/pallas_call | solution.py:83
  74.9 2.0 collective-permute-done
  76.9 2.0 pad_maximum_fusion.2
  79.0 43.2 %all-gather.3.cloned.1.call-done = bf16[8,8,32,896]{3,2,1,0:T(8,128)(2,1)} async-done(((bf16[2,8,32,896]{3,2,1,0:T(8,128)(2,1)}), bf16[8,8,32,896]{3,2,1,0:T(8,128)(2,1)}) %all-gather.3.cloned.1.call-update) | async-done | bytes 3670032 | tf_op jit(solution)/shard_map/all_gather | solution.py:255
  122.1 38.9 %attend.1 = (bf16[512,512]{1,0:T(8,128)(2,1)}, bf16[512,512]{1,0:T(8,128)(2,1)}, f32[2,4,896,128]{3,2,1,0:T(8,128)}) custom-call(s32[1]{0:T(128)} %bitcast.place, bf16[4,2,8,32,896]{4,3,2,1,0:T(8,128)(2,1)} %bitcast.32, bf16[1024,512]{1,0:T(8,128)(2,1)} %queries.1, bf16[1024,512]{1,0:T(8,128)(2,1)} %d_attn.1, bf16[896,512]{1,0:T(8,128)(2,1)} %w_key.1, ...), custom_call_target="tpu_custom_call" | custom-call | flops 8321499136 | bytes 12582912 | tf_op jit(solution)/shard_map/attend/pallas_call | solution.py:187
  161.1 1.8 slice_bitcast_fusion
  163.0 3.8 %collective-permute-done.3 = f32[4,896,128]{2,1,0:T(8,128)S(1)} collective-permute-done((f32[4,896,128]{2,1,0:T(8,128)S(1)}, f32[4,896,128]{2,1,0:T(8,128)S(1)}, u32[]{:S(2)}, u32[]{:S(2)}) %collective-permute-start.3) | collective-permute-done | bytes 1835040 | tf_op jit(solution)/shard_map/ppermute | solution.py:214
  166.9 18.1 %all_to_all.25 = bf16[4,896,128]{2,1,0:T(8,128)(2,1)S(1)} all-to-all(bf16[4,896,128]{2,1,0:T(8,128)(2,1)S(1)} %fusion), channel_id=1, replica_groups=mesh['y'=4,'z'=8,'ret'=2,'tp'=4] {'y'}, dimensions={0} | all-to-all | bytes 1835008 | tf_op jit(solution)/shard_map/all_to_all | solution.py:260
  185.2 17.1 %all_to_all.26 = bf16[8,112,128]{2,1,0:T(8,128)(2,1)S(1)} all-to-all(bf16[8,112,128]{2,1,0:T(8,128)(2,1)S(1)} %bitcast.28), channel_id=1, replica_groups=mesh['y'=4,'z'=8,'ret'=2,'tp'=4] {'z'}, dimensions={0} | all-to-all | bytes 458752 | tf_op jit(solution)/shard_map/all_to_all | solution.py:262
  202.4 12.5 %all_to_all.27 = bf16[8,112,128]{2,1,0:T(8,128)(2,1)S(1)} all-to-all(bf16[8,112,128]{2,1,0:T(8,128)(2,1)S(1)} %broadcast_in_dim.18), channel_id=1, replica_groups=mesh['y'=4,'z'=8,'ret'=2,'tp'=4] {'z'}, dimensions={0} | all-to-all | bytes 458752 | tf_op jit(solution)/shard_map/all_to_all | solution.py:223
  214.9 1.0 broadcast_in_dim.20
  216.0 3.5 %all-to-all-start.4 = ((bf16[4,896,128]{2,1,0:T(8,128)(2,1)}), bf16[4,896,128]{2,1,0:T(8,128)(2,1)S(1)}, u32[]{:S(2)}, u32[]{:S(2)}) async-start(bf16[4,896,128]{2,1,0:T(8,128)(2,1)} %broadcast_in_dim.20), calls=%async_computation.4 | async-start | bytes 1835008 | tf_op jit(solution)/shard_map/all_to_all | solution.py:223
  220.1 9.7 %all-to-all-done.4 = bf16[4,896,128]{2,1,0:T(8,128)(2,1)S(1)} async-done(((bf16[4,896,128]{2,1,0:T(8,128)(2,1)}), bf16[4,896,128]{2,1,0:T(8,128)(2,1)S(1)}, u32[]{:S(2)}, u32[]{:S(2)}) %all-to-all-start.4) | async-done | bytes 917536 | tf_op jit(solution)/shard_map/all_to_all | solution.py:223
  230.6 1.1 broadcast_select_fusion.3
  231.7 1.0 pad_maximum_fusion.1
  232.8 1.0 pad_maximum_fusion
  233.8 1.4 broadcast_select_fusion
  235.2 1.3 copy.20
  236.5 1.3 copy.21
  (29 shorter events, 5.1 us)
Async XLA Ops:
  14.6 56.2 %all-to-all-start = ((bf16[32,32,896]{2,1,0:T(8,128)(2,1)}), bf16[32,32,896]{2,1,0:T(8,128)(2,1)S(1)}, u32[]{:S(2)}, u32[]{:S(2)}) async-start(bf16[32,32,896]{2,1,0:T(8,128)(2,1)} %pack.1), calls=%async_computation | async-start | bytes 3670016 | tf_op jit(solution)/shard_map/all_to_all | solution.py:252
  26.1 96.1 %all-gather.3.cloned.1.call-start = ((), (), s32[]{:S(2)}) async-start(), calls=%async_computation.5 | async-start | bytes 4587520 | tf_op jit(solution)/shard_map/all_gather | solution.py:255
  70.8 1.3 copy-start
  74.8 2.1 collective-permute-start
  161.1 5.7 %copy-start.1 = (f32[2,4,896,128]{3,2,1,0:T(8,128)S(1)}, f32[2,4,896,128]{3,2,1,0:T(8,128)}, u32[]{:S(2)}) copy-start(f32[2,4,896,128]{3,2,1,0:T(8,128)} %get-tuple-element.13) | copy-start | bytes 11010052
  162.9 3.9 %collective-permute-start.3 = (f32[4,896,128]{2,1,0:T(8,128)S(1)}, f32[4,896,128]{2,1,0:T(8,128)S(1)}, u32[]{:S(2)}, u32[]{:S(2)}) collective-permute-start(f32[4,896,128]{2,1,0:T(8,128)S(1)} %slice_bitcast_fusion), channel_id=1, source_target_pairs={{0,4},{4,0},{1,5},{5,1},{2,6},{6,2},{3,7},{7,3},{8,12},{12,8},{9,1... | collective-permute-start | bytes 5505032 | tf_op jit(solution)/shard_map/ppermute | solution.py:214
  185.2 34.3 %copy-start.3 = (bf16[512,512]{1,0:T(8,128)(2,1)S(1)}, bf16[512,512]{1,0:T(8,128)(2,1)}, u32[]{:S(2)}) copy-start(bf16[512,512]{1,0:T(8,128)(2,1)} %get-tuple-element.12) | copy-start | bytes 1572868
  185.2 34.4 %copy-start.2 = (bf16[512,512]{1,0:T(8,128)(2,1)S(1)}, bf16[512,512]{1,0:T(8,128)(2,1)}, u32[]{:S(2)}) copy-start(bf16[512,512]{1,0:T(8,128)(2,1)} %get-tuple-element.11) | copy-start | bytes 1572868
  216.0 13.9 %all-to-all-start.4 = ((bf16[4,896,128]{2,1,0:T(8,128)(2,1)}), bf16[4,896,128]{2,1,0:T(8,128)(2,1)S(1)}, u32[]{:S(2)}, u32[]{:S(2)}) async-start(bf16[4,896,128]{2,1,0:T(8,128)(2,1)} %broadcast_in_dim.20), calls=%async_computation.4 | async-start | bytes 1835008 | tf_op jit(solution)/shard_map/all_to_all | solution.py:223
  219.5 11.1 %collective-permute-start.2 = (bf16[512,512]{1,0:T(8,128)(2,1)S(1)}, bf16[512,512]{1,0:T(8,128)(2,1)}, u32[]{:S(2)}, u32[]{:S(2)}) collective-permute-start(bf16[512,512]{1,0:T(8,128)(2,1)S(1)} %copy-done.3), channel_id=1, source_target_pairs={{0,4},{4,0},{1,5},{5,1},{2,6},{6,2},{3,7},{7,3},{8,12},{12,8},{9,1... | collective-permute-start | bytes 1572872 | tf_op jit(solution)/shard_map/ppermute | solution.py:214
  219.6 13.1 %collective-permute-start.1 = (bf16[512,512]{1,0:T(8,128)(2,1)S(1)}, bf16[512,512]{1,0:T(8,128)(2,1)S(1)}, u32[]{:S(2)}, u32[]{:S(2)}) collective-permute-start(bf16[512,512]{1,0:T(8,128)(2,1)S(1)} %copy-done.2), channel_id=1, source_target_pairs={{0,4},{4,0},{1,5},{5,1},{2,6},{6,2},{3,7},{7,3},{8,12},{12,8},{9,1... | collective-permute-start | bytes 1572872 | tf_op jit(solution)/shard_map/ppermute | solution.py:214
  230.4 3.4 %collective-permute-start.4 = (bf16[4,896,128]{1,2,0:T(8,128)(2,1)S(1)}, bf16[4,896,128]{1,2,0:T(8,128)(2,1)}, u32[]{:S(2)}, u32[]{:S(2)}) collective-permute-start(bf16[4,896,128]{1,2,0:T(8,128)(2,1)S(1)} %copy.18), channel_id=1, source_target_pairs={{0,4},{4,0},{1,5},{5,1},{2,6},{6,2},{3,7},{7,3},{8,12},{12,8},{9,1... | collective-permute-start | bytes 2752520 | tf_op jit(solution)/shard_map/ppermute | solution.py:214
Sparse Core Ops, SparseCore 0:
  79.1 42.9 all-gather.2
